TPU v7x, 32 devices: a whole 2x2x4 slice. The times are simulated.
32 devices in a mesh: dp: 4 (over y, x), expert: 8 (over z, core).
Axes of the slice: x: 2, y: 2, z: 4, core: 2. Of those that a mesh axis runs over, the one named last changes fastest.
Arguments:
- tokens: bfloat16 [4096, 7168], P(('dp', 'expert')), may hold values from -6 to 6
- route_ids: int32 [4096, 8], P(('dp', 'expert')), may hold values from 0 to 255, as said below
- gate_weights: float32 [4096, 8], P(('dp', 'expert')), may hold values from 0.3 to 1.2
- gate_weight: bfloat16 [8, 7168, 1024], P('expert', 'dp'), may hold values from -0.0625 to 0.0625
- up_weight: bfloat16 [8, 7168, 1024], P('expert', 'dp'), may hold values from -0.0625 to 0.0625
- down_weight: bfloat16 [8, 7168, 1024], P('expert', 'dp'), may hold values from -0.1875 to 0.1875
- cotangent: bfloat16 [4096, 7168], P(('dp', 'expert')), may hold values from -3 to 3
Outputs:
- output: bfloat16 [4096, 7168], P(('dp', 'expert'))
- grad_tokens: bfloat16 [4096, 7168], P(('dp', 'expert'))
- grad_gate: bfloat16 [8, 7168, 1024], P('expert', 'dp')
- grad_up: bfloat16 [8, 7168, 1024], P('expert', 'dp')
- grad_down: bfloat16 [8, 7168, 1024], P('expert', 'dp')
Inputs may be any that keep to these rules, and one draw needn't show every extreme that they name: `route_ids`: each token's 8 numbers are different, and at most one of them is below 8. Among the 128 tokens of one device at most 4 name any one number below 8; for each index of dp, one number below 8 is named by exactly 4 tokens of every device with that index.
All inputs are finite; a program needn't handle non-finite values.
Results may differ from a plain program's by a relative error of at most 0.018.
Values may be sent and summed in bfloat16 or wider, within the bound.
No kernel may reach another device: no remote copies, remote signals or barrier semaphores. Data moves between devices by JAX's collectives and lax.ppermute only.
A program may use at most 128 MiB of HBM per device.

v0:
```python
import jax
import jax.numpy as jnp
from jax import lax
from jax.sharding import PartitionSpec as P

CAP = 4


def contract_last(left, right):
    return lax.dot_general(
        left, right, (((1,), (1,)), ((), ())), preferred_element_type=jnp.float32
    )


def contract_first(left, right):
    return lax.dot_general(
        left, right, (((0,), (0,)), ((), ())), preferred_element_type=jnp.float32
    )


def body(tokens, route_ids, gate_weights, gate_weight, up_weight, down_weight, cotangent):
    experts = lax.axis_size("expert")
    gate_mat = gate_weight[0]
    up_mat = up_weight[0]
    down_mat = down_weight[0]
    slice_width = gate_mat.shape[0]
    hidden_units = gate_mat.shape[1]
    labels = jnp.arange(experts, dtype=jnp.int32)
    matches = route_ids[:, :, None] == labels
    chosen = jnp.any(matches, axis=1).astype(jnp.int32)
    gate_of = jnp.sum(jnp.where(matches, gate_weights[:, :, None], 0.0), axis=1)
    ranks = jnp.cumsum(chosen, axis=0) - chosen
    placed = (chosen[:, :, None] == 1) & (ranks[:, :, None] == jnp.arange(CAP, dtype=jnp.int32))
    placer = placed.astype(jnp.bfloat16)
    slot_gate = jnp.sum(jnp.where(placed, gate_of[:, :, None], 0.0), axis=0)
    send_rows = jnp.einsum(
        "tjc,td->jcd", placer, tokens, preferred_element_type=jnp.float32
    ).astype(jnp.bfloat16)
    picked = jnp.einsum("tjc,td->jcd", placer, cotangent, preferred_element_type=jnp.float32)
    send_grads = (slot_gate[:, :, None] * picked).astype(jnp.bfloat16)
    recv_rows, recv_grads = (
        lax.all_to_all(
            lax.all_to_all(send_rows, "dp", split_axis=2, concat_axis=1, tiled=True),
            "expert",
            split_axis=0,
            concat_axis=0,
            tiled=True,
        ),
        lax.all_to_all(
            lax.all_to_all(send_grads, "dp", split_axis=2, concat_axis=1, tiled=True),
            "expert",
            split_axis=0,
            concat_axis=0,
            tiled=True,
        ),
    )
    layout = recv_rows.shape
    row_count = layout[0] * layout[1]
    flat_rows = recv_rows.reshape(row_count, slice_width)
    flat_grads = recv_grads.reshape(row_count, slice_width)
    row_block = flat_rows
    grad_block = flat_grads
    mine = lax.psum_scatter(
        jnp.concatenate(
            [
                jnp.dot(row_block, gate_mat, preferred_element_type=jnp.float32),
                jnp.dot(row_block, up_mat, preferred_element_type=jnp.float32),
                jnp.dot(grad_block, down_mat, preferred_element_type=jnp.float32),
            ],
            axis=1,
        ).astype(jnp.bfloat16),
        "dp",
        scatter_dimension=0,
        tiled=True,
    ).astype(jnp.float32)
    pre_gate = mine[:, :hidden_units]
    pre_up = mine[:, hidden_units : 2 * hidden_units]
    hidden_grad = mine[:, 2 * hidden_units :]
    squash = jax.nn.sigmoid(pre_gate)
    silu_gate = pre_gate * squash
    hidden = (silu_gate * pre_up).astype(jnp.bfloat16)
    gate_grad = (hidden_grad * pre_up * squash * (1.0 + pre_gate * (1.0 - squash))).astype(
        jnp.bfloat16
    )
    up_grad = (hidden_grad * silu_gate).astype(jnp.bfloat16)
    hidden, gate_grad, up_grad = (hidden, gate_grad, up_grad)
    hidden_part = lax.all_gather(hidden, "dp", axis=0, tiled=True)
    gate_part = lax.all_gather(gate_grad, "dp", axis=0, tiled=True)
    up_part = lax.all_gather(up_grad, "dp", axis=0, tiled=True)
    row_block = flat_rows
    grad_block = flat_grads
    out_part = contract_last(hidden_part, down_mat).astype(jnp.bfloat16)
    input_part = (contract_last(gate_part, gate_mat) + contract_last(up_part, up_mat)).astype(
        jnp.bfloat16
    )
    out_rows = out_part
    input_rows = input_part
    gate_total = contract_first(row_block, gate_part)
    up_total = contract_first(row_block, up_part)
    down_total = contract_first(grad_block, hidden_part)
    carry = (out_rows, input_rows, gate_total, up_total, down_total)
    out_rows, input_rows, gate_total, up_total, down_total = carry
    got_out, got_input = (
        lax.all_to_all(
            lax.all_to_all(out_rows.reshape(layout), "dp", split_axis=1, concat_axis=2, tiled=True),
            "expert",
            split_axis=0,
            concat_axis=0,
            tiled=True,
        ),
        lax.all_to_all(
            lax.all_to_all(
                input_rows.reshape(layout), "dp", split_axis=1, concat_axis=2, tiled=True
            ),
            "expert",
            split_axis=0,
            concat_axis=0,
            tiled=True,
        ),
    )
    weighted = slot_gate[:, :, None] * got_out.astype(jnp.float32)
    output = jnp.einsum(
        "tjc,jcd->td", placed.astype(jnp.float32), weighted, precision=lax.Precision.HIGHEST
    ).astype(jnp.bfloat16)
    grad_tokens = jnp.einsum(
        "tjc,jcd->td", placer, got_input, preferred_element_type=jnp.float32
    ).astype(jnp.bfloat16)
    return (
        output,
        grad_tokens,
        gate_total.astype(jnp.bfloat16)[None],
        up_total.astype(jnp.bfloat16)[None],
        down_total.astype(jnp.bfloat16)[None],
    )


def solution(mesh):
    return jax.shard_map(
        body,
        mesh=mesh,
        in_specs=(
            P(("dp", "expert"), None),
            P(("dp", "expert"), None),
            P(("dp", "expert"), None),
            P("expert", "dp", None),
            P("expert", "dp", None),
            P("expert", "dp", None),
            P(("dp", "expert"), None),
        ),
        out_specs=(
            P(("dp", "expert"), None),
            P(("dp", "expert"), None),
            P("expert", "dp", None),
            P("expert", "dp", None),
            P("expert", "dp", None),
        ),
        check_vma=False,
    )
```

profile of v0, /device:TPU:0, one launch (start us, length us, event | category | flops | bytes accessed | tf_op | source)
XLA Modules:
  0.0 243.5 jit_solution(8787925912496322918)
XLA Ops:
  9.1 7.2 %copy.72 = bf16[8,4,7168]{0,1,2:T(4,128)(2,1)} copy(bf16[8,4,7168]{2,0,1:T(8,128)(2,1)S(1)} %convolution_convert_fusion) | data formatting | bytes 917504 | tf_op jit(solution)/shard_map/convert_element_type | solution.py:38
  16.3 10.2 %reshape.53 = bf16[4,2,28672]{2,1,0:T(2,128)(2,1)} reshape(bf16[7168,4,8]{2,1,0:T(4,128)(2,1)} %bitcast.83) | data formatting | bytes 917504
  26.5 5.2 %all-to-all-start = ((bf16[4,2,28672]{2,1,0:T(2,128)(2,1)}), bf16[4,2,28672]{2,1,0:T(2,128)(2,1)S(1)}, u32[]{:S(2)}, u32[]{:S(2)}) async-start(bf16[4,2,28672]{2,1,0:T(2,128)(2,1)} %reshape.53), calls=%async_computation | async-start | bytes 917504 | tf_op jit(solution)/shard_map/all_to_all | solution.py:43
  32.2 7.2 %copy.76 = bf16[8,4,7168]{0,1,2:T(4,128)(2,1)} copy(bf16[8,4,7168]{2,0,1:T(8,128)(2,1)S(1)} %fusion.2) | data formatting | bytes 917504 | tf_op jit(solution)/shard_map/convert_element_type | solution.py:40
  39.4 10.1 %reshape.51 = bf16[4,2,28672]{2,1,0:T(2,128)(2,1)} reshape(bf16[7168,4,8]{2,1,0:T(4,128)(2,1)} %bitcast.84) | data formatting | bytes 917504
  49.5 4.2 %all-to-all-start.2 = ((bf16[4,2,28672]{2,1,0:T(2,128)(2,1)}), bf16[4,2,28672]{2,1,0:T(2,128)(2,1)S(1)}, u32[]{:S(2)}, u32[]{:S(2)}) async-start(bf16[4,2,28672]{2,1,0:T(2,128)(2,1)} %reshape.51), calls=%async_computation.2 | async-start | bytes 917504 | tf_op jit(solution)/shard_map/all_to_all | solution.py:50
  53.6 9.8 %reshape.54 = bf16[7168,4,8]{2,1,0:T(4,128)(2,1)} reshape(bf16[4,2,28672]{2,1,0:T(2,128)(2,1)S(1)} %all-to-all-done) | data formatting | bytes 917504
  63.4 8.7 %copy.74 = bf16[8,4,4,1792]{3,0,2,1:T(8,128)(2,1)S(1)} copy(bf16[8,4,4,1792]{0,2,3,1:T(4,128)(2,1)} %bitcast.85) | data formatting | bytes 917504 | tf_op jit(solution)/shard_map/all_to_all | solution.py:43
  73.0 4.9 %all-to-all-start.1 = ((bf16[8,16,1792]{2,1,0:T(8,128)(2,1)}), bf16[8,16,1792]{2,1,0:T(8,128)(2,1)S(1)}, u32[]{:S(2)}, u32[]{:S(2)}) async-start(bf16[8,16,1792]{2,1,0:T(8,128)(2,1)} %copy.75), calls=%async_computation.1 | async-start | bytes 917504 | tf_op jit(solution)/shard_map/all_to_all | solution.py:42
  77.9 9.8 %reshape.52 = bf16[7168,4,8]{2,1,0:T(4,128)(2,1)} reshape(bf16[4,2,28672]{2,1,0:T(2,128)(2,1)S(1)} %all-to-all-done.2) | data formatting | bytes 917504
  87.7 8.7 %copy.78 = bf16[8,4,4,1792]{3,0,2,1:T(8,128)(2,1)S(1)} copy(bf16[8,4,4,1792]{0,2,3,1:T(4,128)(2,1)} %bitcast.86) | data formatting | bytes 917504 | tf_op jit(solution)/shard_map/all_to_all | solution.py:50
  97.2 5.1 %all-to-all-start.3 = ((bf16[8,16,1792]{2,1,0:T(8,128)(2,1)}), bf16[8,16,1792]{2,1,0:T(8,128)(2,1)S(1)}, u32[]{:S(2)}, u32[]{:S(2)}) async-start(bf16[8,16,1792]{2,1,0:T(8,128)(2,1)} %copy.79), calls=%async_computation.3 | async-start | bytes 917504 | tf_op jit(solution)/shard_map/all_to_all | solution.py:49
  102.3 2.8 %fusion.32 = bf16[128,1024]{1,0:T(8,128)(2,1)S(1)} fusion(bf16[128,1792]{1,0:T(8,128)(2,1)S(1)} %bitcast.87, bf16[1,1792,1024]{2,1,0:T(8,128)(2,1)} %param.11), kind=kOutput, calls=%fused_computation.31 | convolution fusion | flops 469893120 | bytes 4390912 | tf_op jit(solution)/shard_map/dot_general | solution.py:67
  106.1 10.1 %all-to-all-done.3 = bf16[8,16,1792]{2,1,0:T(8,128)(2,1)S(1)} async-done(((bf16[8,16,1792]{2,1,0:T(8,128)(2,1)}), bf16[8,16,1792]{2,1,0:T(8,128)(2,1)S(1)}, u32[]{:S(2)}, u32[]{:S(2)}) %all-to-all-start.3) | async-done | bytes 458784 | tf_op jit(solution)/shard_map/all_to_all | solution.py:49
  116.2 2.7 %fusion.35 = bf16[128,1024]{1,0:T(8,128)(2,1)S(1)} fusion(bf16[128,1792]{1,0:T(8,128)(2,1)S(1)} %bitcast.91, bf16[1,1792,1024]{2,1,0:T(8,128)(2,1)} %param.12), kind=kOutput, calls=%fused_computation.32 | convolution fusion | flops 469893120 | bytes 4390912 | tf_op jit(solution)/shard_map/dot_general | solution.py:68
  119.9 25.7 %reduce-scatter.2.cloned.1.call-done = bf16[32,3072]{1,0:T(8,128)(2,1)} async-done(((bf16[128,3072]{1,0:T(8,128)(2,1)}), bf16[32,3072]{1,0:T(8,128)(2,1)}) %reduce-scatter.2.cloned.1.call-update) | async-done | bytes 196624 | tf_op jit(solution)/shard_map/reduce_scatter | solution.py:63
  146.6 9.1 %all_gather.10 = bf16[128,1024]{1,0:T(8,128)(2,1)S(1)} all-gather(bf16[32,1024]{1,0:T(8,128)(2,1)S(1)} %get-tuple-element.5), channel_id=1, replica_groups=mesh['dp'=4,'expert'=8] {'dp'}, dimensions={0}, use_global_device_ids=true | all-gather | bytes 327680 | tf_op jit(solution)/shard_map/all_gather | solution.py:88
  155.7 8.4 %all_gather.9 = bf16[128,1024]{1,0:T(8,128)(2,1)S(1)} all-gather(bf16[32,1024]{1,0:T(8,128)(2,1)S(1)} %get-tuple-element.6), channel_id=1, replica_groups=mesh['dp'=4,'expert'=8] {'dp'}, dimensions={0}, use_global_device_ids=true | all-gather | bytes 327680 | tf_op jit(solution)/shard_map/all_gather | solution.py:87
  164.1 9.0 %all_gather.11 = bf16[128,1024]{1,0:T(8,128)(2,1)S(1)} all-gather(bf16[32,1024]{1,0:T(8,128)(2,1)S(1)} %get-tuple-element.7), channel_id=1, replica_groups=mesh['dp'=4,'expert'=8] {'dp'}, dimensions={0}, use_global_device_ids=true | all-gather | bytes 327680 | tf_op jit(solution)/shard_map/all_gather | solution.py:89
  173.2 3.4 %fusion.21 = bf16[128,1792]{1,0:T(8,128)(2,1)S(1)} fusion(bf16[128,1024]{1,0:T(8,128)(2,1)S(1)} %all_gather.9, bf16[1,1792,1024]{2,1,0:T(8,128)(2,1)} %param.12), kind=kOutput, calls=%fused_computation.26 | convolution fusion | flops 469991424 | bytes 4390912 | tf_op jit(solution)/shard_map/dot_general | solution.py:10
  177.4 3.5 %all-to-all-start.4 = ((bf16[8,16,1792]{2,0,1:T(8,128)(2,1)}), bf16[8,16,1792]{2,0,1:T(8,128)(2,1)S(1)}, u32[]{:S(2)}, u32[]{:S(2)}) async-start(bf16[8,16,1792]{2,0,1:T(8,128)(2,1)} %copy.80), calls=%async_computation.5 | async-start | bytes 917504 | tf_op jit(solution)/shard_map/all_to_all | solution.py:105
  180.9 3.5 %fusion.7 = f32[128,1792]{1,0:T(8,128)S(1)} fusion(bf16[128,1024]{1,0:T(8,128)(2,1)S(1)} %all_gather.11, bf16[1,1792,1024]{2,1,0:T(8,128)(2,1)} %param.11), kind=kOutput, calls=%fused_computation.14 | convolution fusion | flops 469762048 | bytes 4849664 | tf_op jit(solution)/shard_map/dot_general | solution.py:10
  187.4 3.5 %all-to-all-start.6 = ((bf16[8,16,1792]{2,0,1:T(8,128)(2,1)}), bf16[8,16,1792]{2,0,1:T(8,128)(2,1)S(1)}, u32[]{:S(2)}, u32[]{:S(2)}) async-start(bf16[8,16,1792]{2,0,1:T(8,128)(2,1)} %copy.84), calls=%async_computation.7 | async-start | bytes 917504 | tf_op jit(solution)/shard_map/all_to_all | solution.py:112
  192.2 4.9 %all-to-all-done.6 = bf16[8,16,1792]{2,0,1:T(8,128)(2,1)S(1)} async-done(((bf16[8,16,1792]{2,0,1:T(8,128)(2,1)}), bf16[8,16,1792]{2,0,1:T(8,128)(2,1)S(1)}, u32[]{:S(2)}, u32[]{:S(2)}) %all-to-all-start.6) | async-done | bytes 458784 | tf_op jit(solution)/shard_map/all_to_all | solution.py:112
  197.1 4.6 %all-to-all-start.5 = ((bf16[8,4,7168]{2,1,0:T(4,128)(2,1)}), bf16[8,4,7168]{2,1,0:T(4,128)(2,1)S(1)}, u32[]{:S(2)}, u32[]{:S(2)}) async-start(bf16[8,4,7168]{2,1,0:T(4,128)(2,1)} %reshape.50), calls=%async_computation.6 | async-start | bytes 917504 | tf_op jit(solution)/shard_map/all_to_all | solution.py:104
  203.0 12.6 %all-to-all-done.5 = bf16[8,4,7168]{2,1,0:T(4,128)(2,1)S(1)} async-done(((bf16[8,4,7168]{2,1,0:T(4,128)(2,1)}), bf16[8,4,7168]{2,1,0:T(4,128)(2,1)S(1)}, u32[]{:S(2)}, u32[]{:S(2)}) %all-to-all-start.5) | async-done | bytes 458784 | tf_op jit(solution)/shard_map/all_to_all | solution.py:104
  215.7 4.1 %all-to-all-start.7 = ((bf16[8,4,7168]{2,1,0:T(4,128)(2,1)}), bf16[8,4,7168]{2,1,0:T(4,128)(2,1)}, u32[]{:S(2)}, u32[]{:S(2)}) async-start(bf16[8,4,7168]{2,1,0:T(4,128)(2,1)} %all_to_all.82), calls=%async_computation.8 | async-start | bytes 917504 | tf_op jit(solution)/shard_map/all_to_all | solution.py:111
  219.8 3.0 %fusion.17 = bf16[1,1792,1024]{2,1,0:T(8,128)(2,1)} fusion(bf16[128,1792]{1,0:T(8,128)(2,1)S(1)} %bitcast.92, bf16[128,1024]{1,0:T(8,128)(2,1)S(1)} %all_gather.9), kind=kOutput, calls=%fused_computation.24 | convolution fusion | flops 471597056 | bytes 4390912 | tf_op jit(solution)/shard_map/dot_general | solution.py:16
  222.8 3.0 %fusion.15 = bf16[1,1792,1024]{2,1,0:T(8,128)(2,1)} fusion(bf16[128,1792]{1,0:T(8,128)(2,1)S(1)} %bitcast.89, bf16[128,1024]{1,0:T(8,128)(2,1)S(1)} %all_gather.10), kind=kOutput, calls=%fused_computation.22 | convolution fusion | flops 471597056 | bytes 4390912 | tf_op jit(solution)/shard_map/dot_general | solution.py:16
  225.7 3.0 %fusion.16 = bf16[1,1792,1024]{2,1,0:T(8,128)(2,1)} fusion(bf16[128,1792]{1,0:T(8,128)(2,1)S(1)} %bitcast.90, bf16[128,1024]{1,0:T(8,128)(2,1)S(1)} %all_gather.11), kind=kOutput, calls=%fused_computation.23 | convolution fusion | flops 471597056 | bytes 4390912 | tf_op jit(solution)/shard_map/dot_general | solution.py:16
  228.7 2.9 %fusion = bf16[128,7168]{1,0:T(8,128)(2,1)} fusion(bf16[8,4,7168]{2,1,0:T(4,128)(2,1)S(1)} %all-to-all-done.5, f32[8,4]{0,1:T(4,128)S(1)} %select_reduce_fusion.1, s32[128,8]{0,1:T(8,128)S(1)} %copy.71, pred[128,8]{0,1:T(8,128)(4,1)S(1)} %copy.70), kind=kOutput, calls=%fused_computation.2 | convolution fusion | flops 353705984 | bytes 2299008 | tf_op jit(solution)/shard_map/tjc,jcd->td/dot_general | solution.py:122
  233.7 2.9 %fusion.1 = bf16[128,7168]{1,0:T(8,128)(2,1)} fusion(bf16[8,4,7168]{2,1,0:T(4,128)(2,1)} %all-to-all-done.7, s32[128,8]{0,1:T(8,128)S(1)} %copy.71, pred[128,8]{0,1:T(8,128)(4,1)S(1)} %copy.70), kind=kOutput, calls=%fused_computation.3 | convolution fusion | flops 59645952 | bytes 2298880 | tf_op jit(solution)/shard_map/tjc,jcd->td/dot_general | solution.py:125
  (45 shorter events, 15.5 us)
Async XLA Ops:
  7.2 1.5 copy-start
  16.3 15.4 %copy-start.5 = (s32[128,8]{0,1:T(8,128)S(1)}, s32[128,8]{0,1:T(8,128)}, u32[]{:S(2)}) copy-start(s32[128,8]{0,1:T(8,128)} %param.8) | copy-start | bytes 12292
  16.3 15.4 %copy-start.6 = (f32[128,8]{0,1:T(8,128)S(1)}, f32[128,8]{0,1:T(8,128)}, u32[]{:S(2)}) copy-start(f32[128,8]{0,1:T(8,128)} %param.9) | copy-start | bytes 12292
  16.3 15.5 %copy-start.4 = (bf16[128,7168]{1,0:T(8,128)(2,1)S(1)}, bf16[128,7168]{1,0:T(8,128)(2,1)}, u32[]{:S(2)}) copy-start(bf16[128,7168]{1,0:T(8,128)(2,1)} %param.13) | copy-start | bytes 5505028
  26.5 23.0 %all-to-all-start = ((bf16[4,2,28672]{2,1,0:T(2,128)(2,1)}), bf16[4,2,28672]{2,1,0:T(2,128)(2,1)S(1)}, u32[]{:S(2)}, u32[]{:S(2)}) async-start(bf16[4,2,28672]{2,1,0:T(2,128)(2,1)} %reshape.53), calls=%async_computation | async-start | bytes 917504 | tf_op jit(solution)/shard_map/all_to_all | solution.py:43
  49.5 23.5 %all-to-all-start.2 = ((bf16[4,2,28672]{2,1,0:T(2,128)(2,1)}), bf16[4,2,28672]{2,1,0:T(2,128)(2,1)S(1)}, u32[]{:S(2)}, u32[]{:S(2)}) async-start(bf16[4,2,28672]{2,1,0:T(2,128)(2,1)} %reshape.51), calls=%async_computation.2 | async-start | bytes 917504 | tf_op jit(solution)/shard_map/all_to_all | solution.py:50
  73.0 24.2 %all-to-all-start.1 = ((bf16[8,16,1792]{2,1,0:T(8,128)(2,1)}), bf16[8,16,1792]{2,1,0:T(8,128)(2,1)S(1)}, u32[]{:S(2)}, u32[]{:S(2)}) async-start(bf16[8,16,1792]{2,1,0:T(8,128)(2,1)} %copy.75), calls=%async_computation.1 | async-start | bytes 917504 | tf_op jit(solution)/shard_map/all_to_all | solution.py:42
  97.2 19.0 %all-to-all-start.3 = ((bf16[8,16,1792]{2,1,0:T(8,128)(2,1)}), bf16[8,16,1792]{2,1,0:T(8,128)(2,1)S(1)}, u32[]{:S(2)}, u32[]{:S(2)}) async-start(bf16[8,16,1792]{2,1,0:T(8,128)(2,1)} %copy.79), calls=%async_computation.3 | async-start | bytes 917504 | tf_op jit(solution)/shard_map/all_to_all | solution.py:49
  102.3 43.3 %reduce-scatter.2.cloned.1.call-start = ((), (), s32[]{:S(2)}) async-start(), calls=%async_computation.9 | async-start | bytes 983040 | tf_op jit(solution)/shard_map/reduce_scatter | solution.py:63
  102.3 3.1 %copy-start.2 = (bf16[1,1792,1024]{2,1,0:T(8,128)(2,1)S(1)}, bf16[1,1792,1024]{2,1,0:T(8,128)(2,1)}, u32[]{:S(2)}) copy-start(bf16[1,1792,1024]{2,1,0:T(8,128)(2,1)} %param.10) | copy-start | bytes 11010052
  177.4 9.9 %all-to-all-start.4 = ((bf16[8,16,1792]{2,0,1:T(8,128)(2,1)}), bf16[8,16,1792]{2,0,1:T(8,128)(2,1)S(1)}, u32[]{:S(2)}, u32[]{:S(2)}) async-start(bf16[8,16,1792]{2,0,1:T(8,128)(2,1)} %copy.80), calls=%async_computation.5 | async-start | bytes 917504 | tf_op jit(solution)/shard_map/all_to_all | solution.py:105
  180.9 3.5 %copy-start.3 = (bf16[1,1792,1024]{2,1,0:T(8,128)(2,1)S(1)}, bf16[1,1792,1024]{2,1,0:T(8,128)(2,1)}, u32[]{:S(2)}) copy-start(bf16[1,1792,1024]{2,1,0:T(8,128)(2,1)} %param.10) | copy-start | bytes 11010052
  187.4 9.8 %all-to-all-start.6 = ((bf16[8,16,1792]{2,0,1:T(8,128)(2,1)}), bf16[8,16,1792]{2,0,1:T(8,128)(2,1)S(1)}, u32[]{:S(2)}, u32[]{:S(2)}) async-start(bf16[8,16,1792]{2,0,1:T(8,128)(2,1)} %copy.84), calls=%async_computation.7 | async-start | bytes 917504 | tf_op jit(solution)/shard_map/all_to_all | solution.py:112
  197.1 18.5 %all-to-all-start.5 = ((bf16[8,4,7168]{2,1,0:T(4,128)(2,1)}), bf16[8,4,7168]{2,1,0:T(4,128)(2,1)S(1)}, u32[]{:S(2)}, u32[]{:S(2)}) async-start(bf16[8,4,7168]{2,1,0:T(4,128)(2,1)} %reshape.50), calls=%async_computation.6 | async-start | bytes 917504 | tf_op jit(solution)/shard_map/all_to_all | solution.py:104
  215.7 18.1 %all-to-all-start.7 = ((bf16[8,4,7168]{2,1,0:T(4,128)(2,1)}), bf16[8,4,7168]{2,1,0:T(4,128)(2,1)}, u32[]{:S(2)}, u32[]{:S(2)}) async-start(bf16[8,4,7168]{2,1,0:T(4,128)(2,1)} %all_to_all.82), calls=%async_computation.8 | async-start | bytes 917504 | tf_op jit(solution)/shard_map/all_to_all | solution.py:111
  222.8 13.9 %copy-start.1 = (bf16[128,7168]{1,0:T(8,128)(2,1)S(1)}, bf16[128,7168]{1,0:T(8,128)(2,1)}, u32[]{:S(2)}) copy-start(bf16[128,7168]{1,0:T(8,128)(2,1)} %param.7) | copy-start | bytes 5505028
Sparse Core Ops, SparseCore 0:
  120.0 25.5 reduce-scatter.1
where the time goes:
time: 245 us; the launch traced here: 243 us
  local copies, waits for them, and re-layouts  78.5 us (32%)
  waiting for transfers between devices  56.1 us (23%)
  starting transfers between devices  35.1 us (14%)
  matrix products  29.9 us (12%)
  blocking collectives  26.5 us (11%)
  between operations  14.2 us (6%)
  other arithmetic  3.11 us (1%)
    unnamed x18, local copies, waits for them, and re-layouts  40.4 us
    reduce_scatter x1, waiting for transfers between devices, body(): lax.psum_scatter(jnp.concatenate([jnp.dot(row_block, gate_mat, preferred_...  25.7 us
    all_to_all x1, waiting for transfers between devices, body(): lax.all_to_all(lax.all_to_all(out_rows.reshape(layout), 'dp', split_axis=...  12.6 us
    all_to_all x1, waiting for transfers between devices, body(): lax.all_to_all(lax.all_to_all(send_grads, 'dp', split_axis=2, concat_axis...  10.1 us
    all_to_all x2, local copies, waits for them, and re-layouts, body(): lax.all_to_all(send_rows, 'dp', split_axis=2, concat_axis=1, tiled=True)  9.54 us
    all_to_all x2, local copies, waits for them, and re-layouts, body(): lax.all_to_all(send_grads, 'dp', split_axis=2, concat_axis=1, tiled=True)  9.54 us
    all_gather x1, blocking collectives, body(): gate_part = lax.all_gather(gate_grad, 'dp', axis=0, tiled=True)  9.05 us
    all_gather x1, blocking collectives, body(): up_part = lax.all_gather(up_grad, 'dp', axis=0, tiled=True)  9.04 us
  transfers between devices with their start and end apart: 9, of which 6 were waited for; matrix products, arithmetic and copies ran while one was open for 33% of the time, Pallas kernels for 0%

commit v1 on v0

--- a/solution.py
+++ b/solution.py
@@ -4,6 +4,30 @@
 from jax.sharding import PartitionSpec as P
 
 CAP = 4
+
+
+def split_up(x, dim, size):
+    lengths = x.shape
+    blocks = x.reshape(*lengths[:dim], size, lengths[dim] // size, *lengths[dim + 1 :])
+    return jnp.moveaxis(blocks, dim, 0)
+
+
+def laid_out(parts, dim):
+    shape = list(parts.shape[1:])
+    shape[dim] *= parts.shape[0]
+    return jnp.moveaxis(parts, 0, dim).reshape(shape)
+
+
+def sent_to_each(value, axis, split_dim, concat_dim):
+    size, index = (lax.axis_size(axis), lax.axis_index(axis))
+    blocks = split_up(value, split_dim, size)
+    out = blocks
+    for step in range(1, size):
+        target, source = ((index + step) % size, (index - step) % size)
+        sent = lax.dynamic_index_in_dim(blocks, target, 0)
+        theirs = lax.ppermute(sent, axis, [(i, (i + step) % size) for i in range(size)])
+        out = lax.dynamic_update_slice_in_dim(out, theirs, source, axis=0)
+    return laid_out(out, concat_dim)
 
 
 def contract_last(left, right):
@@ -47,11 +71,7 @@
             tiled=True,
         ),
         lax.all_to_all(
-            lax.all_to_all(send_grads, "dp", split_axis=2, concat_axis=1, tiled=True),
-            "expert",
-            split_axis=0,
-            concat_axis=0,
-            tiled=True,
+            sent_to_each(send_grads, "dp", 2, 1), "expert", split_axis=0, concat_axis=0, tiled=True
         ),
     )
     layout = recv_rows.shape

time: 245 us -> 221 us (0.902)
  local copies, waits for them, and re-layouts: 78.5 us -> 51.5 us
  waiting for transfers between devices: 56.1 us -> 52.5 us
    unnamed x18 -> x8, local copies, waits for them, and re-layouts: 40.4 us -> 20.2 us
    all_to_all x1, waiting for transfers between devices: 0.01 us -> 11.2 us  [body(): lax.all_to_all(lax.all_to_all(send_rows, 'dp', split_axis=2, concat_axis=...]
    all_to_all x1, waiting for transfers between devices: 12.6 us -> 2.06 us  [body(): lax.all_to_all(lax.all_to_all(out_rows.reshape(layout), 'dp', split_axis=...]
    all_to_all x2 -> x1, waiting for transfers between devices: 10.1 us -> 0.01 us  [body(): lax.all_to_all(sent_to_each(send_grads, 'dp', 2, 1), 'expert', split_axis...]
    all_to_all x2 -> x0, local copies, waits for them, and re-layouts: 9.54 us -> none  [body(): lax.all_to_all(send_grads, 'dp', split_axis=2, concat_axis=1, tiled=True)]
    all_to_all x1, waiting for transfers between devices: 2.05 us -> 9.93 us  [body(): lax.all_to_all(lax.all_to_all(input_rows.reshape(layout), 'dp', split_axi...]
    convert_element_type x1 -> x0, local copies, waits for them, and re-layouts: 7.2 us -> none  [body(): send_grads = (slot_gate[:, :, None] * picked).astype(jnp.bfloat16)]
    ppermute x0 -> x3, starting transfers between devices: none -> 5.92 us  [sent_to_each(): lax.ppermute(sent, axis, [(i, (i + step) % size) for i in range(size)])]
  transfers between devices with their start and end apart: 9 -> 11, of which waited for: 6 -> 6; matrix products, arithmetic and copies ran while one was open for 33% -> 31% of each run, Pallas kernels for 0% -> 0%
where the time goes in v1:
time: 221 us; the launch traced here: 219 us
  waiting for transfers between devices  52.5 us (24%)
  local copies, waits for them, and re-layouts  51.5 us (23%)
  starting transfers between devices  36.5 us (17%)
  matrix products  32.3 us (15%)
  blocking collectives  27.6 us (12%)
  between operations  14.3 us (6%)
  other arithmetic  4.6 us (2%)
    reduce_scatter x1, waiting for transfers between devices, body(): lax.psum_scatter(jnp.concatenate([jnp.dot(row_block, gate_mat, preferred_...  24.3 us
    unnamed x8, local copies, waits for them, and re-layouts  20.2 us
    all_to_all x1, waiting for transfers between devices, body(): lax.all_to_all(lax.all_to_all(send_rows, 'dp', split_axis=2, concat_axis=...  11.2 us
    all_gather x1, blocking collectives, body(): hidden_part = lax.all_gather(hidden, 'dp', axis=0, tiled=True)  10.6 us
    all_to_all x1, waiting for transfers between devices, body(): lax.all_to_all(lax.all_to_all(input_rows.reshape(layout), 'dp', split_axi...  9.93 us
    all_to_all x2, local copies, waits for them, and re-layouts, body(): lax.all_to_all(send_rows, 'dp', split_axis=2, concat_axis=1, tiled=True)  9.54 us
    all_gather x1, blocking collectives, body(): up_part = lax.all_gather(up_grad, 'dp', axis=0, tiled=True)  9.04 us
    dot_general x3, matrix products, contract_first(): lax.dot_general(left, right, (((0,), (0,)), ((), ())), preferred_element_...  8.94 us
  transfers between devices with their start and end apart: 11, of which 6 were waited for; matrix products, arithmetic and copies ran while one was open for 31% of the time, Pallas kernels for 0%

profile of v1, /device:TPU:0, one launch (start us, length us, event | category | flops | bytes accessed | tf_op | source)
XLA Modules:
  0.0 219.3 jit_solution(5409831113310534493)
XLA Ops:
  10.4 3.0 %collective-permute-start = (bf16[1,8,4,1792]{3,1,2,0:T(8,128)(2,1)}, bf16[1,8,4,1792]{3,1,2,0:T(8,128)(2,1)}, u32[]{:S(2)}, u32[]{:S(2)}) collective-permute-start(bf16[1,8,4,1792]{3,1,2,0:T(8,128)(2,1)} %get-tuple-element.7), channel_id=1, source_target_pairs={{0,8},{8,16},{16,24},{24,0},{1,9},{9,17},{17,25},{25,1},{2,10},{10... | collective-permute-start | bytes 344072 | tf_op jit(solution)/shard_map/ppermute | solution.py:28
  18.2 7.2 %copy.70 = bf16[8,4,7168]{0,1,2:T(4,128)(2,1)} copy(bf16[8,4,7168]{2,0,1:T(8,128)(2,1)S(1)} %convolution_convert_fusion) | data formatting | bytes 917504 | tf_op jit(solution)/shard_map/convert_element_type | solution.py:62
  25.4 10.1 %reshape.62 = bf16[4,2,28672]{2,1,0:T(2,128)(2,1)} reshape(bf16[7168,4,8]{2,1,0:T(4,128)(2,1)} %bitcast.89) | data formatting | bytes 917504
  35.5 3.5 %all-to-all-start = ((bf16[4,2,28672]{2,1,0:T(2,128)(2,1)}), bf16[4,2,28672]{2,1,0:T(2,128)(2,1)S(1)}, u32[]{:S(2)}, u32[]{:S(2)}) async-start(bf16[4,2,28672]{2,1,0:T(2,128)(2,1)} %reshape.62), calls=%async_computation | async-start | bytes 917504 | tf_op jit(solution)/shard_map/all_to_all | solution.py:67
  42.7 3.0 %all-to-all-done = bf16[4,2,28672]{2,1,0:T(2,128)(2,1)S(1)} async-done(((bf16[4,2,28672]{2,1,0:T(2,128)(2,1)}), bf16[4,2,28672]{2,1,0:T(2,128)(2,1)S(1)}, u32[]{:S(2)}, u32[]{:S(2)}) %all-to-all-start) | async-done | bytes 458784 | tf_op jit(solution)/shard_map/all_to_all | solution.py:67
  45.7 4.9 %all-to-all-start.2 = ((bf16[8,16,1792]{2,1,0:T(8,128)(2,1)}), bf16[8,16,1792]{2,1,0:T(8,128)(2,1)S(1)}, u32[]{:S(2)}, u32[]{:S(2)}) async-start(bf16[8,16,1792]{2,1,0:T(8,128)(2,1)} %copy.75), calls=%async_computation.2 | async-start | bytes 917504 | tf_op jit(solution)/shard_map/all_to_all | solution.py:73
  50.6 9.8 %reshape.63 = bf16[7168,4,8]{2,1,0:T(4,128)(2,1)} reshape(bf16[4,2,28672]{2,1,0:T(2,128)(2,1)S(1)} %all-to-all-done) | data formatting | bytes 917504
  60.3 8.7 %copy.72 = bf16[8,4,4,1792]{3,0,2,1:T(8,128)(2,1)S(1)} copy(bf16[8,4,4,1792]{0,2,3,1:T(4,128)(2,1)} %bitcast.90) | data formatting | bytes 917504 | tf_op jit(solution)/shard_map/all_to_all | solution.py:67
  69.9 5.1 %all-to-all-start.1 = ((bf16[8,16,1792]{2,1,0:T(8,128)(2,1)}), bf16[8,16,1792]{2,1,0:T(8,128)(2,1)S(1)}, u32[]{:S(2)}, u32[]{:S(2)}) async-start(bf16[8,16,1792]{2,1,0:T(8,128)(2,1)} %copy.73), calls=%async_computation.1 | async-start | bytes 917504 | tf_op jit(solution)/shard_map/all_to_all | solution.py:66
  75.0 2.7 %fusion.35 = bf16[128,1024]{1,0:T(8,128)(2,1)S(1)} fusion(bf16[128,1792]{1,0:T(8,128)(2,1)S(1)} %bitcast.95, bf16[1,1792,1024]{2,1,0:T(8,128)(2,1)} %param.12), kind=kOutput, calls=%fused_computation.32 | convolution fusion | flops 469893120 | bytes 4390912 | tf_op jit(solution)/shard_map/dot_general | solution.py:88
  77.7 11.2 %all-to-all-done.1 = bf16[8,16,1792]{2,1,0:T(8,128)(2,1)S(1)} async-done(((bf16[8,16,1792]{2,1,0:T(8,128)(2,1)}), bf16[8,16,1792]{2,1,0:T(8,128)(2,1)S(1)}, u32[]{:S(2)}, u32[]{:S(2)}) %all-to-all-start.1) | async-done | bytes 458784 | tf_op jit(solution)/shard_map/all_to_all | solution.py:66
  88.9 2.8 %fusion.29 = bf16[128,1024]{1,0:T(8,128)(2,1)S(1)} fusion(bf16[128,1792]{1,0:T(8,128)(2,1)S(1)} %bitcast.91, bf16[1,1792,1024]{2,1,0:T(8,128)(2,1)} %param.10), kind=kOutput, calls=%fused_computation.30 | convolution fusion | flops 469893120 | bytes 4390912 | tf_op jit(solution)/shard_map/dot_general | solution.py:86
  93.7 24.3 %reduce-scatter.2.cloned.1.call-done = bf16[32,3072]{1,0:T(8,128)(2,1)} async-done(((bf16[128,3072]{1,0:T(8,128)(2,1)}), bf16[32,3072]{1,0:T(8,128)(2,1)}) %reduce-scatter.2.cloned.1.call-update) | async-done | bytes 196624 | tf_op jit(solution)/shard_map/reduce_scatter | solution.py:83
  119.8 9.0 %all_gather.11 = bf16[128,1024]{1,0:T(8,128)(2,1)S(1)} all-gather(bf16[32,1024]{1,0:T(8,128)(2,1)S(1)} %get-tuple-element.10), channel_id=1, replica_groups=mesh['dp'=4,'expert'=8] {'dp'}, dimensions={0}, use_global_device_ids=true | all-gather | bytes 327680 | tf_op jit(solution)/shard_map/all_gather | solution.py:109
  128.8 7.9 %all_gather.10 = bf16[128,1024]{1,0:T(8,128)(2,1)S(1)} all-gather(bf16[32,1024]{1,0:T(8,128)(2,1)S(1)} %get-tuple-element.8), channel_id=1, replica_groups=mesh['dp'=4,'expert'=8] {'dp'}, dimensions={0}, use_global_device_ids=true | all-gather | bytes 327680 | tf_op jit(solution)/shard_map/all_gather | solution.py:108
  136.7 3.4 %fusion.7 = f32[128,1792]{1,0:T(8,128)S(1)} fusion(bf16[128,1024]{1,0:T(8,128)(2,1)S(1)} %all_gather.11, bf16[1,1792,1024]{2,1,0:T(8,128)(2,1)} %param.11), kind=kOutput, calls=%fused_computation.14 | convolution fusion | flops 469762048 | bytes 4849664 | tf_op jit(solution)/shard_map/dot_general | solution.py:34
  142.4 4.1 %all-to-all-start.5 = ((bf16[8,16,1792]{2,0,1:T(8,128)(2,1)}), bf16[8,16,1792]{2,0,1:T(8,128)(2,1)}, u32[]{:S(2)}, u32[]{:S(2)}) async-start(bf16[8,16,1792]{2,0,1:T(8,128)(2,1)} %copy.80), calls=%async_computation.6 | async-start | bytes 917504 | tf_op jit(solution)/shard_map/all_to_all | solution.py:132
  146.5 10.6 %all_gather.9 = bf16[128,1024]{1,0:T(8,128)(2,1)S(1)} all-gather(bf16[32,1024]{1,0:T(8,128)(2,1)} %get-tuple-element.9), channel_id=1, replica_groups=mesh['dp'=4,'expert'=8] {'dp'}, dimensions={0}, use_global_device_ids=true | all-gather | bytes 327680 | tf_op jit(solution)/shard_map/all_gather | solution.py:107
  157.2 3.4 %fusion.21 = bf16[128,1792]{1,0:T(8,128)(2,1)S(1)} fusion(bf16[128,1024]{1,0:T(8,128)(2,1)S(1)} %all_gather.9, bf16[1,1792,1024]{2,1,0:T(8,128)(2,1)} %param.12), kind=kOutput, calls=%fused_computation.26 | convolution fusion | flops 469991424 | bytes 4390912 | tf_op jit(solution)/shard_map/dot_general | solution.py:34
  161.4 4.3 %all-to-all-start.3 = ((bf16[8,16,1792]{2,0,1:T(8,128)(2,1)}), bf16[8,16,1792]{2,0,1:T(8,128)(2,1)}, u32[]{:S(2)}, u32[]{:S(2)}) async-start(bf16[8,16,1792]{2,0,1:T(8,128)(2,1)} %copy.76), calls=%async_computation.4 | async-start | bytes 917504 | tf_op jit(solution)/shard_map/all_to_all | solution.py:125
  165.7 2.1 copy.81
  169.8 2.0 all-to-all-done.3
  171.9 4.6 %all-to-all-start.6 = ((bf16[8,4,7168]{2,1,0:T(4,128)(2,1)}), bf16[8,4,7168]{2,1,0:T(4,128)(2,1)}, u32[]{:S(2)}, u32[]{:S(2)}) async-start(bf16[8,4,7168]{2,1,0:T(4,128)(2,1)} %all_to_all.65), calls=%async_computation.7 | async-start | bytes 917504 | tf_op jit(solution)/shard_map/all_to_all | solution.py:131
  176.5 2.1 copy.85
  180.6 9.9 %all-to-all-done.6 = bf16[8,4,7168]{2,1,0:T(4,128)(2,1)} async-done(((bf16[8,4,7168]{2,1,0:T(4,128)(2,1)}), bf16[8,4,7168]{2,1,0:T(4,128)(2,1)}, u32[]{:S(2)}, u32[]{:S(2)}) %all-to-all-start.6) | async-done | bytes 458784 | tf_op jit(solution)/shard_map/all_to_all | solution.py:131
  190.5 4.1 %all-to-all-start.4 = ((bf16[8,4,7168]{2,1,0:T(4,128)(2,1)}), bf16[8,4,7168]{2,1,0:T(4,128)(2,1)}, u32[]{:S(2)}, u32[]{:S(2)}) async-start(bf16[8,4,7168]{2,1,0:T(4,128)(2,1)} %reshape.61), calls=%async_computation.5 | async-start | bytes 917504 | tf_op jit(solution)/shard_map/all_to_all | solution.py:124
  194.6 3.0 %fusion.16 = bf16[1,1792,1024]{2,1,0:T(8,128)(2,1)} fusion(bf16[128,1792]{1,0:T(8,128)(2,1)S(1)} %bitcast.93, bf16[128,1024]{1,0:T(8,128)(2,1)S(1)} %all_gather.11), kind=kOutput, calls=%fused_computation.23 | convolution fusion | flops 471597056 | bytes 4390912 | tf_op jit(solution)/shard_map/dot_general | solution.py:40
  197.6 3.0 %fusion.15 = bf16[1,1792,1024]{2,1,0:T(8,128)(2,1)} fusion(bf16[128,1792]{1,0:T(8,128)(2,1)S(1)} %bitcast.94, bf16[128,1024]{1,0:T(8,128)(2,1)S(1)} %all_gather.10), kind=kOutput, calls=%fused_computation.22 | convolution fusion | flops 471597056 | bytes 4390912 | tf_op jit(solution)/shard_map/dot_general | solution.py:40
  200.6 3.0 %fusion.17 = bf16[1,1792,1024]{2,1,0:T(8,128)(2,1)} fusion(bf16[128,1792]{1,0:T(8,128)(2,1)S(1)} %bitcast.96, bf16[128,1024]{1,0:T(8,128)(2,1)S(1)} %all_gather.9), kind=kOutput, calls=%fused_computation.24 | convolution fusion | flops 471597056 | bytes 4390912 | tf_op jit(solution)/shard_map/dot_general | solution.py:40
  203.6 2.9 %fusion.1 = bf16[128,7168]{1,0:T(8,128)(2,1)} fusion(bf16[8,4,7168]{2,1,0:T(4,128)(2,1)} %all-to-all-done.6, s32[128,8]{0,1:T(8,128)S(1)} %copy.69, pred[128,8]{0,1:T(8,128)(4,1)S(1)} %copy.68), kind=kOutput, calls=%fused_computation.3 | convolution fusion | flops 59645952 | bytes 2298880 | tf_op jit(solution)/shard_map/tjc,jcd->td/dot_general | solution.py:145
  206.5 2.1 all-to-all-done.4
  208.5 3.9 %fusion = bf16[128,7168]{1,0:T(8,128)(2,1)} fusion(bf16[8,4,7168]{2,1,0:T(4,128)(2,1)} %all-to-all-done.4, f32[8,4]{0,1:T(4,128)S(1)} %select_reduce_fusion.1, s32[128,8]{0,1:T(8,128)S(1)} %copy.69, pred[128,8]{0,1:T(8,128)(4,1)S(1)} %copy.68), kind=kOutput, calls=%fused_computation.2 | convolution fusion | flops 353705984 | bytes 2299008 | tf_op jit(solution)/shard_map/tjc,jcd->td/dot_general | solution.py:142
  (42 shorter events, 23.3 us)
Async XLA Ops:
  7.2 2.2 copy-start
  10.4 28.7 %collective-permute-start = (bf16[1,8,4,1792]{3,1,2,0:T(8,128)(2,1)}, bf16[1,8,4,1792]{3,1,2,0:T(8,128)(2,1)}, u32[]{:S(2)}, u32[]{:S(2)}) collective-permute-start(bf16[1,8,4,1792]{3,1,2,0:T(8,128)(2,1)} %get-tuple-element.7), channel_id=1, source_target_pairs={{0,8},{8,16},{16,24},{24,0},{1,9},{9,17},{17,25},{25,1},{2,10},{10... | collective-permute-start | bytes 344072 | tf_op jit(solution)/shard_map/ppermute | solution.py:28
  13.4 26.6 %collective-permute-start.1 = (bf16[1,8,4,1792]{3,1,2,0:T(8,128)(2,1)S(1)}, bf16[1,8,4,1792]{3,1,2,0:T(8,128)(2,1)}, u32[]{:S(2)}, u32[]{:S(2)}) collective-permute-start(bf16[1,8,4,1792]{3,1,2,0:T(8,128)(2,1)S(1)} %get-tuple-element.6), channel_id=1, source_target_pairs={{0,16},{8,24},{16,0},{24,8},{1,17},{9,25},{17,1},{25,9},{2,18},{10... | collective-permute-start | bytes 344072 | tf_op jit(solution)/shard_map/ppermute | solution.py:28
  14.9 26.0 %collective-permute-start.2 = (bf16[1,8,4,1792]{3,1,2,0:T(8,128)(2,1)S(1)}, bf16[1,8,4,1792]{3,1,2,0:T(8,128)(2,1)}, u32[]{:S(2)}, u32[]{:S(2)}) collective-permute-start(bf16[1,8,4,1792]{3,1,2,0:T(8,128)(2,1)S(1)} %get-tuple-element.5), channel_id=1, source_target_pairs={{0,24},{8,0},{16,8},{24,16},{1,25},{9,1},{17,9},{25,17},{2,26},{10... | collective-permute-start | bytes 344072 | tf_op jit(solution)/shard_map/ppermute | solution.py:28
  35.5 10.2 %all-to-all-start = ((bf16[4,2,28672]{2,1,0:T(2,128)(2,1)}), bf16[4,2,28672]{2,1,0:T(2,128)(2,1)S(1)}, u32[]{:S(2)}, u32[]{:S(2)}) async-start(bf16[4,2,28672]{2,1,0:T(2,128)(2,1)} %reshape.62), calls=%async_computation | async-start | bytes 917504 | tf_op jit(solution)/shard_map/all_to_all | solution.py:67
  45.7 24.2 %all-to-all-start.2 = ((bf16[8,16,1792]{2,1,0:T(8,128)(2,1)}), bf16[8,16,1792]{2,1,0:T(8,128)(2,1)S(1)}, u32[]{:S(2)}, u32[]{:S(2)}) async-start(bf16[8,16,1792]{2,1,0:T(8,128)(2,1)} %copy.75), calls=%async_computation.2 | async-start | bytes 917504 | tf_op jit(solution)/shard_map/all_to_all | solution.py:73
  69.9 19.0 %all-to-all-start.1 = ((bf16[8,16,1792]{2,1,0:T(8,128)(2,1)}), bf16[8,16,1792]{2,1,0:T(8,128)(2,1)S(1)}, u32[]{:S(2)}, u32[]{:S(2)}) async-start(bf16[8,16,1792]{2,1,0:T(8,128)(2,1)} %copy.73), calls=%async_computation.1 | async-start | bytes 917504 | tf_op jit(solution)/shard_map/all_to_all | solution.py:66
  75.0 43.0 %reduce-scatter.2.cloned.1.call-start = ((), (), s32[]{:S(2)}) async-start(), calls=%async_computation.8 | async-start | bytes 983040 | tf_op jit(solution)/shard_map/reduce_scatter | solution.py:83
  88.9 3.1 %copy-start.1 = (bf16[1,1792,1024]{2,1,0:T(8,128)(2,1)S(1)}, bf16[1,1792,1024]{2,1,0:T(8,128)(2,1)}, u32[]{:S(2)}) copy-start(bf16[1,1792,1024]{2,1,0:T(8,128)(2,1)} %param.11) | copy-start | bytes 11010052
  118.0 22.2 %copy-start.2 = (bf16[1,1792,1024]{2,1,0:T(8,128)(2,1)S(1)}, bf16[1,1792,1024]{2,1,0:T(8,128)(2,1)}, u32[]{:S(2)}) copy-start(bf16[1,1792,1024]{2,1,0:T(8,128)(2,1)} %param.10) | copy-start | bytes 11010052
  142.4 19.1 %all-to-all-start.5 = ((bf16[8,16,1792]{2,0,1:T(8,128)(2,1)}), bf16[8,16,1792]{2,0,1:T(8,128)(2,1)}, u32[]{:S(2)}, u32[]{:S(2)}) async-start(bf16[8,16,1792]{2,0,1:T(8,128)(2,1)} %copy.80), calls=%async_computation.6 | async-start | bytes 917504 | tf_op jit(solution)/shard_map/all_to_all | solution.py:132
  161.4 10.4 %all-to-all-start.3 = ((bf16[8,16,1792]{2,0,1:T(8,128)(2,1)}), bf16[8,16,1792]{2,0,1:T(8,128)(2,1)}, u32[]{:S(2)}, u32[]{:S(2)}) async-start(bf16[8,16,1792]{2,0,1:T(8,128)(2,1)} %copy.76), calls=%async_computation.4 | async-start | bytes 917504 | tf_op jit(solution)/shard_map/all_to_all | solution.py:125
  171.9 18.6 %all-to-all-start.6 = ((bf16[8,4,7168]{2,1,0:T(4,128)(2,1)}), bf16[8,4,7168]{2,1,0:T(4,128)(2,1)}, u32[]{:S(2)}, u32[]{:S(2)}) async-start(bf16[8,4,7168]{2,1,0:T(4,128)(2,1)} %all_to_all.65), calls=%async_computation.7 | async-start | bytes 917504 | tf_op jit(solution)/shard_map/all_to_all | solution.py:131
  190.5 18.1 %all-to-all-start.4 = ((bf16[8,4,7168]{2,1,0:T(4,128)(2,1)}), bf16[8,4,7168]{2,1,0:T(4,128)(2,1)}, u32[]{:S(2)}, u32[]{:S(2)}) async-start(bf16[8,4,7168]{2,1,0:T(4,128)(2,1)} %reshape.61), calls=%async_computation.5 | async-start | bytes 917504 | tf_op jit(solution)/shard_map/all_to_all | solution.py:124
Sparse Core Ops, SparseCore 0:
  93.8 24.1 reduce-scatter.1
